TPU v7x, 32 devices: a whole 2x2x4 slice. The times are simulated.
32 devices in a mesh: dp: 8 (over y, x, core), tensor: 4 (over z).
Axes of the slice: x: 2, y: 2, z: 4, core: 2. Of those that a mesh axis runs over, the one named last changes fastest.
Arguments:
- send_order: int32 [32, 32], P(('dp', 'tensor')), may hold values from 0 to 31, each once within a row
- master: float32 [32, 32, 2048], P(('dp', 'tensor')), may hold values from -6 to 6
- first_code: bfloat16 [32, 32, 2048], P(('dp', 'tensor')), may hold values from -1 to 1
- first_scale: float32 [32, 32], P(('dp', 'tensor')), may hold values from 0.1 to 2
- second_code: bfloat16 [32, 32, 2048], P(('dp', 'tensor')), may hold values from 0.049804688 to 1
- second_scale: float32 [32, 32], P(('dp', 'tensor')), may hold values from 0.5 to 20
- grads: bfloat16 [8, 4, 8, 32, 2048], P('dp', 'tensor'), may hold values from -6 to 6
Outputs:
- new_master: float32 [32, 32, 2048], P(('dp', 'tensor'))
- new_first_code: bfloat16 [32, 32, 2048], P(('dp', 'tensor'))
- new_first_scale: float32 [32, 32], P(('dp', 'tensor'))
- new_second_code: bfloat16 [32, 32, 2048], P(('dp', 'tensor'))
- new_second_scale: float32 [32, 32], P(('dp', 'tensor'))
- weights: bfloat16 [4, 8, 32, 2048], P('tensor')
Inputs may be any that keep to these rules, and one draw needn't show every extreme that they name: `send_order`: each row is an ordering of the slots 0 to 31, each once.
All inputs are finite; a program needn't handle non-finite values. Where the computation divides by a largest or mean magnitude, that divisor is 1e-20 or more.
Results may differ from a plain program's by a relative error of at most 0.001.
Values may be sent and summed in bfloat16 or wider, within the bound.
A program may use at most 128 MiB of HBM per device.

v0:
```python
import jax
import jax.numpy as jnp
from jax import lax
from jax.sharding import PartitionSpec as P

STEP = 10


def on_device(send_order, master, first_code, first_scale, second_code, second_scale, grads):
    count_dp = lax.axis_size("dp")
    count_tensor = lax.axis_size("tensor")
    devices_all = count_dp * count_tensor
    slots = master.shape[1]
    width = master.shape[2]
    per_peer = slots // devices_all
    order_row = send_order[0]
    moved = (
        master[0][order_row],
        first_code[0][order_row],
        first_scale[0][order_row],
        second_code[0][order_row],
        second_scale[0][order_row],
    )
    shaped = tuple((item.reshape((devices_all, per_peer) + item.shape[1:]) for item in moved))
    arrived = (
        lax.all_to_all(shaped[0], ("dp", "tensor"), split_axis=0, concat_axis=0, tiled=True),
        lax.all_to_all(
            shaped[1].astype(jnp.float32), ("dp", "tensor"), split_axis=0, concat_axis=0, tiled=True
        ).astype(jnp.bfloat16),
        lax.all_to_all(shaped[2], ("dp", "tensor"), split_axis=0, concat_axis=0, tiled=True),
        lax.all_to_all(
            shaped[3].astype(jnp.float32), ("dp", "tensor"), split_axis=0, concat_axis=0, tiled=True
        ).astype(jnp.bfloat16),
        lax.all_to_all(shaped[4], ("dp", "tensor"), split_axis=0, concat_axis=0, tiled=True),
    )
    master_new = arrived[0].reshape(slots, width)
    code_one = arrived[1].reshape(slots, width)
    scale_one = arrived[2].reshape(slots)
    code_two = arrived[3].reshape(slots, width)
    scale_two = arrived[4].reshape(slots)
    summed = lax.psum_scatter(grads.astype(jnp.float32), "dp", scatter_dimension=2, tiled=True)
    grad = summed.reshape(slots, width)
    first = code_one.astype(jnp.float32) * scale_one[:, None]
    second = code_two.astype(jnp.float32) * scale_two[:, None]
    moment_one = 0.9 * first + 0.1 * grad
    moment_two = 0.95 * second + 0.05 * grad * grad
    corr_one = 1.0 - 0.9**STEP
    corr_two = 1.0 - 0.95**STEP
    update = moment_one / corr_one / (jnp.sqrt(moment_two / corr_two) + 1e-08) + 0.1 * master_new
    new_master = master_new - 0.01 * update
    new_scale_one = jnp.max(jnp.abs(moment_one), axis=1) + 1e-06
    new_code_one = (moment_one / new_scale_one[:, None]).astype(jnp.bfloat16)
    new_scale_two = jnp.max(jnp.abs(moment_two), axis=1) + 1e-06
    new_code_two = (moment_two / new_scale_two[:, None]).astype(jnp.bfloat16)
    local_weights = new_master.astype(jnp.bfloat16).reshape(1, 1, slots, width)
    weights = lax.all_gather(local_weights, "dp", axis=1, tiled=True)
    return (
        new_master.reshape(1, slots, width),
        new_code_one.reshape(1, slots, width),
        new_scale_one.reshape(1, slots),
        new_code_two.reshape(1, slots, width),
        new_scale_two.reshape(1, slots),
        weights,
    )


def solution(mesh):
    placed = (
        P(("dp", "tensor"), None),
        P(("dp", "tensor"), None, None),
        P(("dp", "tensor"), None, None),
        P(("dp", "tensor"), None),
        P(("dp", "tensor"), None, None),
        P(("dp", "tensor"), None),
        P("dp", "tensor", None, None, None),
    )
    return jax.shard_map(
        on_device,
        mesh=mesh,
        in_specs=placed,
        out_specs=(
            P(("dp", "tensor"), None, None),
            P(("dp", "tensor"), None, None),
            P(("dp", "tensor"), None),
            P(("dp", "tensor"), None, None),
            P(("dp", "tensor"), None),
            P("tensor", None, None, None),
        ),
        check_vma=False,
    )
```

profile of v0, /device:TPU:0, one launch (start us, length us, event | category | flops | bytes accessed | tf_op | source)
XLA Modules:
  0.0 104.7 jit_solution(7902596441690301470)
XLA Ops:
  7.2 2.9 %bitcast_convert_fusion = f32[1,1,8,32,2048]{4,3,1,0,2:T(8,128)} fusion(bf16[1,1,8,32,2048]{4,3,2,1,0:T(8,128)(2,1)} %param.13), kind=kLoop, calls=%fused_computation.5 | loop fusion | flops 524288 | bytes 3145728 | tf_op jit(solution)/shard_map/convert_element_type | solution.py:41
  10.2 0.7 gather_fusion.4
  10.9 0.7 copy.43
  11.6 7.3 %all-to-all-start.4 = ((f32[32,1,1]{2,1,0:T(1,128)}), f32[32,1,1]{2,1,0:T(1,128)S(1)}, u32[]{:S(2)}, u32[]{:S(2)}) async-start(f32[32,1,1]{2,1,0:T(1,128)} %copy.43), calls=%async_computation.5 | async-start | bytes 32768 | tf_op jit(solution)/shard_map/all_to_all | solution.py:34
  18.9 0.7 gather_fusion.3
  19.6 0.7 gather_fusion.2
  20.3 0.7 copy.40
  21.0 5.0 %all-to-all-done.4 = f32[32,1,1]{2,1,0:T(1,128)S(1)} async-done(((f32[32,1,1]{2,1,0:T(1,128)}), f32[32,1,1]{2,1,0:T(1,128)S(1)}, u32[]{:S(2)}, u32[]{:S(2)}) %all-to-all-start.4) | async-done | bytes 160 | tf_op jit(solution)/shard_map/all_to_all | solution.py:34
  26.0 2.5 %all-to-all-start.2 = ((f32[32,1,1]{2,1,0:T(1,128)}), f32[32,1,1]{2,1,0:T(1,128)S(1)}, u32[]{:S(2)}, u32[]{:S(2)}) async-start(f32[32,1,1]{2,1,0:T(1,128)} %copy.40), calls=%async_computation.2 | async-start | bytes 32768 | tf_op jit(solution)/shard_map/all_to_all | solution.py:30
  28.6 0.5 broadcast.345
  29.1 0.7 reduce.2
  29.8 0.7 reshape.649
  30.5 5.2 %all-to-all-done.2 = f32[32,1,1]{2,1,0:T(1,128)S(1)} async-done(((f32[32,1,1]{2,1,0:T(1,128)}), f32[32,1,1]{2,1,0:T(1,128)S(1)}, u32[]{:S(2)}, u32[]{:S(2)}) %all-to-all-start.2) | async-done | bytes 160 | tf_op jit(solution)/shard_map/all_to_all | solution.py:30
  35.7 2.6 %all-to-all-start.3 = ((bf16[32,2,1024]{2,1,0:T(2,128)(2,1)}), bf16[32,2,1024]{2,1,0:T(2,128)(2,1)S(1)}, u32[]{:S(2)}, u32[]{:S(2)}) async-start(bf16[32,2,1024]{2,1,0:T(2,128)(2,1)} %reshape.649), calls=%async_computation.4 | async-start | bytes 262144 | tf_op jit(solution)/shard_map/all_to_all | solution.py:31
  38.3 0.7 gather_fusion.1
  39.0 0.7 reduce.3
  39.6 0.7 reshape.647
  40.4 6.3 %all-to-all-done.3 = bf16[32,2,1024]{2,1,0:T(2,128)(2,1)S(1)} async-done(((bf16[32,2,1024]{2,1,0:T(2,128)(2,1)}), bf16[32,2,1024]{2,1,0:T(2,128)(2,1)S(1)}, u32[]{:S(2)}, u32[]{:S(2)}) %all-to-all-start.3) | async-done | bytes 131104 | tf_op jit(solution)/shard_map/all_to_all | solution.py:31
  46.7 2.6 %all-to-all-start.1 = ((bf16[32,2,1024]{2,1,0:T(2,128)(2,1)}), bf16[32,2,1024]{2,1,0:T(2,128)(2,1)S(1)}, u32[]{:S(2)}, u32[]{:S(2)}) async-start(bf16[32,2,1024]{2,1,0:T(2,128)(2,1)} %reshape.647), calls=%async_computation.1 | async-start | bytes 262144 | tf_op jit(solution)/shard_map/all_to_all | solution.py:27
  49.3 0.7 gather_fusion
  49.9 1.0 copy.37
  50.9 6.7 %all-to-all-done.1 = bf16[32,2,1024]{2,1,0:T(2,128)(2,1)S(1)} async-done(((bf16[32,2,1024]{2,1,0:T(2,128)(2,1)}), bf16[32,2,1024]{2,1,0:T(2,128)(2,1)S(1)}, u32[]{:S(2)}, u32[]{:S(2)}) %all-to-all-start.1) | async-done | bytes 131104 | tf_op jit(solution)/shard_map/all_to_all | solution.py:27
  57.6 2.6 %all-to-all-start = ((f32[32,1,2048]{2,1,0:T(1,128)}), f32[32,1,2048]{2,1,0:T(1,128)S(1)}, u32[]{:S(2)}, u32[]{:S(2)}) async-start(f32[32,1,2048]{2,1,0:T(1,128)} %copy.37), calls=%async_computation | async-start | bytes 524288 | tf_op jit(solution)/shard_map/all_to_all | solution.py:26
  60.3 0.3 reduce.1
  61.2 9.2 %all-to-all-done = f32[32,1,2048]{2,1,0:T(1,128)S(1)} async-done(((f32[32,1,2048]{2,1,0:T(1,128)}), f32[32,1,2048]{2,1,0:T(1,128)S(1)}, u32[]{:S(2)}, u32[]{:S(2)}) %all-to-all-start) | async-done | bytes 262176 | tf_op jit(solution)/shard_map/all_to_all | solution.py:26
  70.5 2.8 %fusion.24 = bf16[1,1,32,2048]{3,0,2,1:T(2,128)(2,1)S(1)} fusion(f32[1,1,1,32,2048]{4,3,1,0,2:T(8,128)} %reduce-scatter.2.cloned.1.call-done, f32[1,1,32,2048]{3,2,1,0:T(8,128)S(1)} %get-tuple-element.26, f32[32,1,2048]{2,1,0:T(1,128)S(1)} %all-to-all-done, f32[32]{0:T(128)S(1)} %reduce.1, bf16[32,1,2048]{2,1,0:T(2,128)(2,1)S(1)} %reshape.650), kind=kLoop, calls=%fused_computation.50 | loop fusion | flops 1114112 | bytes 1048704 | tf_op jit(solution)/shard_map/convert_element_type | solution.py:55
  73.3 0.7 copy.45
  74.3 0.3 fusion.3
  74.7 0.5 fusion.26
  75.2 1.2 %divide_convert_fusion = (bf16[1,32,2048]{2,1,0:T(8,128)(2,1)}, f32[1,32,2048]{2,1,0:T(8,128)}, bf16[1,32,2048]{2,1,0:T(8,128)(2,1)}) fusion(f32[32]{0:T(128)S(1)} %get-tuple-element.35, f32[1,1,1,32,2048]{4,3,1,0,2:T(8,128)S(1)} %copy-done.5, f32[32,1,2048]{2,1,0:T(1,128)S(1)} %convert_element_type.203, f32[32]{0:T(128)S(1)} %reduce.1, f32[32]{0:T(128)S(1)} %reduce, ...), kind=kLoop, calls=%fused_computation.47 | loop fusion | flops 1441792 | bytes 1442304 | tf_op jit(solution)/shard_map/convert_element_type | solution.py:54
  76.4 19.2 %all-gather.2.cloned.1.call-done = bf16[1,8,32,2048]{3,2,0,1:T(8,128)(2,1)} async-done(((bf16[1,1,32,2048]{3,2,0,1:T(8,128)(2,1)}), bf16[1,8,32,2048]{3,2,0,1:T(8,128)(2,1)}) %all-gather.2.cloned.1.call-update) | async-done | bytes 1048592 | tf_op jit(solution)/shard_map/all_gather | solution.py:56
  95.6 2.3 %copy.72 = bf16[1,8,32,2048]{3,2,1,0:T(8,128)(2,1)} copy(bf16[1,8,32,2048]{3,2,1,0:T(8,128)(2,1)} %bitcast.131) | data formatting | bytes 2097152
  (26 shorter events, 1.0 us)
Async XLA Ops:
  7.2 42.1 %copy-start = (f32[1,32,2048]{2,1,0:T(8,128)S(1)}, f32[1,32,2048]{2,1,0:T(8,128)}, u32[]{:S(2)}) copy-start(f32[1,32,2048]{2,1,0:T(8,128)} %param.8) | copy-start | bytes 786436
  7.2 3.0 %copy-start.6 = (s32[1,32]{1,0:T(1,128)S(1)}, s32[1,32]{1,0:T(1,128)}, u32[]{:S(2)}) copy-start(s32[1,32]{1,0:T(1,128)} %param.7) | copy-start | bytes 388
  7.2 3.0 %copy-start.1 = (f32[1,32]{1,0:T(1,128)S(1)}, f32[1,32]{1,0:T(1,128)}, u32[]{:S(2)}) copy-start(f32[1,32]{1,0:T(1,128)} %param.12) | copy-start | bytes 388
  7.2 63.3 %reduce-scatter.2.cloned.1.call-start = ((), (), s32[]{:S(2)}) async-start(), calls=%async_computation.6 | async-start | bytes 2359296 | tf_op jit(solution)/shard_map/reduce_scatter | solution.py:41
  10.1 8.8 %copy-start.3 = (bf16[1,32,2048]{2,1,0:T(8,128)(2,1)S(1)}, bf16[1,32,2048]{2,1,0:T(8,128)(2,1)}, u32[]{:S(2)}) copy-start(bf16[1,32,2048]{2,1,0:T(8,128)(2,1)} %param.11) | copy-start | bytes 393220
  10.1 9.5 %copy-start.2 = (f32[1,32]{1,0:T(1,128)S(1)}, f32[1,32]{1,0:T(1,128)}, u32[]{:S(2)}) copy-start(f32[1,32]{1,0:T(1,128)} %param.10) | copy-start | bytes 388
  10.1 28.2 %copy-start.4 = (bf16[1,32,2048]{2,1,0:T(8,128)(2,1)S(1)}, bf16[1,32,2048]{2,1,0:T(8,128)(2,1)}, u32[]{:S(2)}) copy-start(bf16[1,32,2048]{2,1,0:T(8,128)(2,1)} %param.9) | copy-start | bytes 393220
  11.6 14.5 %all-to-all-start.4 = ((f32[32,1,1]{2,1,0:T(1,128)}), f32[32,1,1]{2,1,0:T(1,128)S(1)}, u32[]{:S(2)}, u32[]{:S(2)}) async-start(f32[32,1,1]{2,1,0:T(1,128)} %copy.43), calls=%async_computation.5 | async-start | bytes 32768 | tf_op jit(solution)/shard_map/all_to_all | solution.py:34
  26.0 9.7 %all-to-all-start.2 = ((f32[32,1,1]{2,1,0:T(1,128)}), f32[32,1,1]{2,1,0:T(1,128)S(1)}, u32[]{:S(2)}, u32[]{:S(2)}) async-start(f32[32,1,1]{2,1,0:T(1,128)} %copy.40), calls=%async_computation.2 | async-start | bytes 32768 | tf_op jit(solution)/shard_map/all_to_all | solution.py:30
  35.7 11.0 %all-to-all-start.3 = ((bf16[32,2,1024]{2,1,0:T(2,128)(2,1)}), bf16[32,2,1024]{2,1,0:T(2,128)(2,1)S(1)}, u32[]{:S(2)}, u32[]{:S(2)}) async-start(bf16[32,2,1024]{2,1,0:T(2,128)(2,1)} %reshape.649), calls=%async_computation.4 | async-start | bytes 262144 | tf_op jit(solution)/shard_map/all_to_all | solution.py:31
  46.7 11.0 %all-to-all-start.1 = ((bf16[32,2,1024]{2,1,0:T(2,128)(2,1)}), bf16[32,2,1024]{2,1,0:T(2,128)(2,1)S(1)}, u32[]{:S(2)}, u32[]{:S(2)}) async-start(bf16[32,2,1024]{2,1,0:T(2,128)(2,1)} %reshape.647), calls=%async_computation.1 | async-start | bytes 262144 | tf_op jit(solution)/shard_map/all_to_all | solution.py:27
  57.6 12.8 %all-to-all-start = ((f32[32,1,2048]{2,1,0:T(1,128)}), f32[32,1,2048]{2,1,0:T(1,128)S(1)}, u32[]{:S(2)}, u32[]{:S(2)}) async-start(f32[32,1,2048]{2,1,0:T(1,128)} %copy.37), calls=%async_computation | async-start | bytes 524288 | tf_op jit(solution)/shard_map/all_to_all | solution.py:26
  60.2 35.3 %all-gather.2.cloned.1.call-start = ((), (), s32[]{:S(2)}) async-start(), calls=%async_computation.7 | async-start | bytes 1179648 | tf_op jit(solution)/shard_map/all_gather | solution.py:56
  70.5 3.8 %copy-start.5 = (f32[1,1,1,32,2048]{4,3,1,0,2:T(8,128)S(1)}, f32[1,1,1,32,2048]{4,3,1,0,2:T(8,128)}, u32[]{:S(2)}) copy-start(f32[1,1,1,32,2048]{4,3,1,0,2:T(8,128)} %reduce-scatter.2.cloned.1.call-done) | copy-start | bytes 786436
Sparse Core Ops, SparseCore 0:
  11.3 46.3 reduce-scatter.1
  74.1 21.3 all-gather.1
where the time goes:
time: 105 us
  waiting for transfers between devices  51.7 us (49%)
  starting transfers between devices  17.7 us (17%)
  between operations  14.2 us (14%)
  local copies, waits for them, and re-layouts  11 us (10%)
  other arithmetic  10.1 us (10%)
    all_gather x1, waiting for transfers between devices, on_device(): weights = lax.all_gather(local_weights, 'dp', axis=1, tiled=True)  19.2 us
    all_to_all x1, waiting for transfers between devices, on_device(): lax.all_to_all(shaped[0], ('dp', 'tensor'), split_axis=0, concat_axis=0,...  9.21 us
    all_to_all x1, starting transfers between devices, on_device(): lax.all_to_all(shaped[4], ('dp', 'tensor'), split_axis=0, concat_axis=0,...  7.33 us
    all_to_all x1, waiting for transfers between devices, on_device(): lax.all_to_all(shaped[1].astype(jnp.float32), ('dp', 'tensor'), split_axi...  6.73 us
    all_to_all x1, waiting for transfers between devices, on_device(): lax.all_to_all(shaped[3].astype(jnp.float32), ('dp', 'tensor'), split_axi...  6.3 us
    all_to_all x1, waiting for transfers between devices, on_device(): lax.all_to_all(shaped[2], ('dp', 'tensor'), split_axis=0, concat_axis=0,...  5.2 us
    all_to_all x1, waiting for transfers between devices, on_device(): lax.all_to_all(shaped[4], ('dp', 'tensor'), split_axis=0, concat_axis=0,...  5.05 us
    unnamed x19, local copies, waits for them, and re-layouts  4 us
  transfers between devices with their start and end apart: 7, of which 6 were waited for; matrix products, arithmetic and copies ran while one was open for 12% of the time, Pallas kernels for 0%

commit v1 on v0

--- a/solution.py
+++ b/solution.py
@@ -4,6 +4,27 @@
 from jax.sharding import PartitionSpec as P
 
 STEP = 10
+
+
+def gather_around(x, axis, dim):
+    length, position, span = (lax.axis_size(axis), lax.axis_index(axis), x.shape[dim])
+    right = [(i, (i + 1) % length) for i in range(length)]
+    left = [(i, (i - 1) % length) for i in range(length)]
+    result = jnp.zeros((*x.shape[:dim], length * span, *x.shape[dim + 1 :]), x.dtype)
+    result = lax.dynamic_update_slice_in_dim(result, x, position * span, axis=dim)
+    from_left = from_right = x
+    halfway = length // 2
+    for step in range(1, halfway + 1):
+        from_left = lax.ppermute(from_left, axis, right)
+        result = lax.dynamic_update_slice_in_dim(
+            result, from_left, (position - step) % length * span, axis=dim
+        )
+        if step < length - halfway:
+            from_right = lax.ppermute(from_right, axis, left)
+            result = lax.dynamic_update_slice_in_dim(
+                result, from_right, (position + step) % length * span, axis=dim
+            )
+    return result
 
 
 def on_device(send_order, master, first_code, first_scale, second_code, second_scale, grads):
@@ -53,7 +74,7 @@
     new_scale_two = jnp.max(jnp.abs(moment_two), axis=1) + 1e-06
     new_code_two = (moment_two / new_scale_two[:, None]).astype(jnp.bfloat16)
     local_weights = new_master.astype(jnp.bfloat16).reshape(1, 1, slots, width)
-    weights = lax.all_gather(local_weights, "dp", axis=1, tiled=True)
+    weights = gather_around(local_weights, "dp", 1)
     return (
         new_master.reshape(1, slots, width),
         new_code_one.reshape(1, slots, width),

time: 105 us -> 115 us (1.095)
  starting transfers between devices: 17.7 us -> 25.6 us
  waiting for transfers between devices: 51.7 us -> 53.6 us
  local copies, waits for them, and re-layouts: 11 us -> 9.67 us
    ppermute x0 -> x7, waiting for transfers between devices: none -> 21.5 us  [the longest x4 20.9 us: gather_around(): from_left = lax.ppermute(from_left, axis, right)]
    all_gather x1 -> x0, waiting for transfers between devices: 19.2 us -> none  [on_device(): weights = lax.all_gather(local_weights, 'dp', axis=1, tiled=True)]
    ppermute x0 -> x7, starting transfers between devices: none -> 7.99 us  [the longest x3 7.59 us: gather_around(): from_right = lax.ppermute(from_right, axis, left)]
    unnamed x19 -> x20, local copies, waits for them, and re-layouts: 4 us -> 2.66 us
  transfers between devices with their start and end apart: 7 -> 13, of which waited for: 6 -> 10; matrix products, arithmetic and copies ran while one was open for 12% -> 12% of each run, Pallas kernels for 0% -> 0%
where the time goes in v1:
time: 115 us; the launch traced here: 114 us
  waiting for transfers between devices  53.6 us (47%)
  starting transfers between devices  25.6 us (22%)
  between operations  14.4 us (13%)
  other arithmetic  11 us (10%)
  local copies, waits for them, and re-layouts  9.67 us (8%)
    ppermute x4, waiting for transfers between devices, gather_around(): from_left = lax.ppermute(from_left, axis, right)  20.9 us
    all_to_all x1, waiting for transfers between devices, on_device(): lax.all_to_all(shaped[0], ('dp', 'tensor'), split_axis=0, concat_axis=0,...  8.86 us
    ppermute x3, starting transfers between devices, gather_around(): from_right = lax.ppermute(from_right, axis, left)  7.59 us
    all_to_all x1, starting transfers between devices, on_device(): lax.all_to_all(shaped[4], ('dp', 'tensor'), split_axis=0, concat_axis=0,...  7.33 us
    all_to_all x1, waiting for transfers between devices, on_device(): lax.all_to_all(shaped[1].astype(jnp.float32), ('dp', 'tensor'), split_axi...  6.73 us
    all_to_all x1, waiting for transfers between devices, on_device(): lax.all_to_all(shaped[3].astype(jnp.float32), ('dp', 'tensor'), split_axi...  6.3 us
    all_to_all x1, waiting for transfers between devices, on_device(): lax.all_to_all(shaped[2], ('dp', 'tensor'), split_axis=0, concat_axis=0,...  5.2 us
    all_to_all x1, waiting for transfers between devices, on_device(): lax.all_to_all(shaped[4], ('dp', 'tensor'), split_axis=0, concat_axis=0,...  5.05 us
  transfers between devices with their start and end apart: 13, of which 10 were waited for; matrix products, arithmetic and copies ran while one was open for 12% of the time, Pallas kernels for 0%

profile of v1, /device:TPU:0, one launch (start us, length us, event | category | flops | bytes accessed | tf_op | source)
XLA Modules:
  0.0 114.4 jit_solution(1938217730490275275)
XLA Ops:
  7.2 2.8 %bitcast_convert_fusion = f32[1,1,8,32,2048]{4,3,1,0,2:T(8,128)} fusion(bf16[1,1,8,32,2048]{4,3,2,1,0:T(8,128)(2,1)} %param.13), kind=kLoop, calls=%fused_computation.5 | loop fusion | flops 524288 | bytes 3145728 | tf_op jit(solution)/shard_map/convert_element_type | solution.py:62
  10.2 0.7 gather_fusion.4
  10.9 0.7 copy.55
  11.6 7.3 %all-to-all-start.4 = ((f32[32,1,1]{2,1,0:T(1,128)}), f32[32,1,1]{2,1,0:T(1,128)S(1)}, u32[]{:S(2)}, u32[]{:S(2)}) async-start(f32[32,1,1]{2,1,0:T(1,128)} %copy.55), calls=%async_computation.5 | async-start | bytes 32768 | tf_op jit(solution)/shard_map/all_to_all | solution.py:55
  19.6 0.7 gather_fusion.2
  20.3 0.7 copy.52
  21.0 5.0 %all-to-all-done.4 = f32[32,1,1]{2,1,0:T(1,128)S(1)} async-done(((f32[32,1,1]{2,1,0:T(1,128)}), f32[32,1,1]{2,1,0:T(1,128)S(1)}, u32[]{:S(2)}, u32[]{:S(2)}) %all-to-all-start.4) | async-done | bytes 160 | tf_op jit(solution)/shard_map/all_to_all | solution.py:55
  26.0 2.5 %all-to-all-start.2 = ((f32[32,1,1]{2,1,0:T(1,128)}), f32[32,1,1]{2,1,0:T(1,128)S(1)}, u32[]{:S(2)}, u32[]{:S(2)}) async-start(f32[32,1,1]{2,1,0:T(1,128)} %copy.52), calls=%async_computation.2 | async-start | bytes 32768 | tf_op jit(solution)/shard_map/all_to_all | solution.py:51
  29.1 0.7 reduce.2
  29.8 0.7 reshape.649
  30.5 5.2 %all-to-all-done.2 = f32[32,1,1]{2,1,0:T(1,128)S(1)} async-done(((f32[32,1,1]{2,1,0:T(1,128)}), f32[32,1,1]{2,1,0:T(1,128)S(1)}, u32[]{:S(2)}, u32[]{:S(2)}) %all-to-all-start.2) | async-done | bytes 160 | tf_op jit(solution)/shard_map/all_to_all | solution.py:51
  35.7 2.6 %all-to-all-start.3 = ((bf16[32,2,1024]{2,1,0:T(2,128)(2,1)}), bf16[32,2,1024]{2,1,0:T(2,128)(2,1)S(1)}, u32[]{:S(2)}, u32[]{:S(2)}) async-start(bf16[32,2,1024]{2,1,0:T(2,128)(2,1)} %reshape.649), calls=%async_computation.4 | async-start | bytes 262144 | tf_op jit(solution)/shard_map/all_to_all | solution.py:52
  38.9 0.7 reduce.3
  39.6 0.7 reshape.647
  40.4 6.3 %all-to-all-done.3 = bf16[32,2,1024]{2,1,0:T(2,128)(2,1)S(1)} async-done(((bf16[32,2,1024]{2,1,0:T(2,128)(2,1)}), bf16[32,2,1024]{2,1,0:T(2,128)(2,1)S(1)}, u32[]{:S(2)}, u32[]{:S(2)}) %all-to-all-start.3) | async-done | bytes 131104 | tf_op jit(solution)/shard_map/all_to_all | solution.py:52
  46.7 2.6 %all-to-all-start.1 = ((bf16[32,2,1024]{2,1,0:T(2,128)(2,1)}), bf16[32,2,1024]{2,1,0:T(2,128)(2,1)S(1)}, u32[]{:S(2)}, u32[]{:S(2)}) async-start(bf16[32,2,1024]{2,1,0:T(2,128)(2,1)} %reshape.647), calls=%async_computation.1 | async-start | bytes 262144 | tf_op jit(solution)/shard_map/all_to_all | solution.py:48
  49.2 0.7 gather_fusion
  49.9 1.0 copy.49
  50.9 6.7 %all-to-all-done.1 = bf16[32,2,1024]{2,1,0:T(2,128)(2,1)S(1)} async-done(((bf16[32,2,1024]{2,1,0:T(2,128)(2,1)}), bf16[32,2,1024]{2,1,0:T(2,128)(2,1)S(1)}, u32[]{:S(2)}, u32[]{:S(2)}) %all-to-all-start.1) | async-done | bytes 131104 | tf_op jit(solution)/shard_map/all_to_all | solution.py:48
  57.6 2.6 %all-to-all-start = ((f32[32,1,2048]{2,1,0:T(1,128)}), f32[32,1,2048]{2,1,0:T(1,128)S(1)}, u32[]{:S(2)}, u32[]{:S(2)}) async-start(f32[32,1,2048]{2,1,0:T(1,128)} %copy.49), calls=%async_computation | async-start | bytes 524288 | tf_op jit(solution)/shard_map/all_to_all | solution.py:47
  61.6 8.9 %all-to-all-done = f32[32,1,2048]{2,1,0:T(1,128)S(1)} async-done(((f32[32,1,2048]{2,1,0:T(1,128)}), f32[32,1,2048]{2,1,0:T(1,128)S(1)}, u32[]{:S(2)}, u32[]{:S(2)}) %all-to-all-start) | async-done | bytes 262176 | tf_op jit(solution)/shard_map/all_to_all | solution.py:47
  70.4 2.8 %fusion.24 = bf16[1,1,32,2048]{3,0,2,1:T(2,128)(2,1)S(1)} fusion(f32[1,1,1,32,2048]{4,3,1,0,2:T(8,128)} %reduce-scatter.2.cloned.1.call-done, f32[1,1,32,2048]{3,2,1,0:T(8,128)S(1)} %get-tuple-element.8, f32[32,1,2048]{2,1,0:T(1,128)S(1)} %all-to-all-done, f32[32]{0:T(128)S(1)} %reduce.1, bf16[32,1,2048]{2,1,0:T(2,128)(2,1)S(1)} %reshape.650), kind=kLoop, calls=%fused_computation.50 | loop fusion | flops 1114112 | bytes 1048704 | tf_op jit(solution)/shard_map/convert_element_type | solution.py:76
  73.6 2.3 %collective-permute-start.1 = (bf16[1,1,32,2048]{3,0,2,1:T(2,128)(2,1)S(1)}, bf16[1,1,32,2048]{3,0,2,1:T(2,128)(2,1)S(1)}, u32[]{:S(2)}, u32[]{:S(2)}) collective-permute-start(bf16[1,1,32,2048]{3,0,2,1:T(2,128)(2,1)S(1)} %fusion.24), channel_id=1, source_target_pairs={{0,28},{4,0},{8,4},{12,8},{16,12},{20,16},{24,20},{28,24},{1,29},{... | collective-permute-start | bytes 393224 | tf_op jit(solution)/shard_map/ppermute | solution.py:23
  75.9 1.3 %fusion.3 = (f32[32]{0:T(128)S(1)}, f32[32]{0:T(128)S(1)}) fusion(f32[1,1,1,32,2048]{4,3,1,0,2:T(8,128)} %reduce-scatter.2.cloned.1.call-done, f32[32,1,2048]{2,1,0:T(1,128)S(1)} %convert_element_type.203, f32[32]{0:T(128)S(1)} %reduce.1, f32[32]{0:T(128)S(1)} %reduce, bf16[32,1,2048]{2,0,1:T(8,128)(2,1)S(1)} %get-tuple-element.9), kind=kLoop, calls=%fused_computation.15 | loop fusion | flops 917440 | bytes 655872 | tf_op jit(solution)/shard_map/reduce_max | solution.py:74
  77.7 1.2 %divide_convert_fusion = (bf16[1,32,2048]{2,1,0:T(8,128)(2,1)}, f32[1,32,2048]{2,1,0:T(8,128)}, bf16[1,32,2048]{2,1,0:T(8,128)(2,1)}) fusion(f32[32]{0:T(128)S(1)} %get-tuple-element.17, f32[1,1,1,32,2048]{4,3,1,0,2:T(8,128)S(1)} %copy-done.5, f32[32,1,2048]{2,1,0:T(1,128)S(1)} %convert_element_type.203, f32[32]{0:T(128)S(1)} %reduce.1, f32[32]{0:T(128)S(1)} %reduce, ...), kind=kLoop, calls=%fused_computation.47 | loop fusion | flops 1441792 | bytes 1442304 | tf_op jit(solution)/shard_map/convert_element_type | solution.py:75
  79.2 3.3 %collective-permute-done = bf16[1,1,32,2048]{3,0,2,1:T(2,128)(2,1)S(1)} collective-permute-done((bf16[1,1,32,2048]{3,0,2,1:T(2,128)(2,1)S(1)}, bf16[1,1,32,2048]{3,0,2,1:T(2,128)(2,1)S(1)}, u32[]{:S(2)}, u32[]{:S(2)}) %collective-permute-start) | collective-permute-done | bytes 131104 | tf_op jit(solution)/shard_map/ppermute | solution.py:18
  82.5 2.6 %collective-permute-start.3 = (bf16[1,1,32,2048]{3,0,2,1:T(2,128)(2,1)S(1)}, bf16[1,1,32,2048]{3,0,2,1:T(2,128)(2,1)S(1)}, u32[]{:S(2)}, u32[]{:S(2)}) collective-permute-start(bf16[1,1,32,2048]{3,0,2,1:T(2,128)(2,1)S(1)} %collective-permute-done.1), channel_id=1, source_target_pairs={{0,28},{4,0},{8,4},{12,8},{16,12},{20,16},{24,20},{28,24},{1,29},{... | collective-permute-start | bytes 393224 | tf_op jit(solution)/shard_map/ppermute | solution.py:23
  85.3 6.1 %collective-permute-done.2 = bf16[1,1,32,2048]{3,0,2,1:T(2,128)(2,1)S(1)} collective-permute-done((bf16[1,1,32,2048]{3,0,2,1:T(2,128)(2,1)S(1)}, bf16[1,1,32,2048]{3,0,2,1:T(2,128)(2,1)S(1)}, u32[]{:S(2)}, u32[]{:S(2)}) %collective-permute-start.2) | collective-permute-done | bytes 131104 | tf_op jit(solution)/shard_map/ppermute | solution.py:18
  91.4 2.6 %collective-permute-start.5 = (bf16[1,1,32,2048]{3,0,2,1:T(2,128)(2,1)S(1)}, bf16[1,1,32,2048]{3,0,2,1:T(2,128)(2,1)S(1)}, u32[]{:S(2)}, u32[]{:S(2)}) collective-permute-start(bf16[1,1,32,2048]{3,0,2,1:T(2,128)(2,1)S(1)} %collective-permute-done.3), channel_id=1, source_target_pairs={{0,28},{4,0},{8,4},{12,8},{16,12},{20,16},{24,20},{28,24},{1,29},{... | collective-permute-start | bytes 393224 | tf_op jit(solution)/shard_map/ppermute | solution.py:23
  94.2 5.5 %collective-permute-done.4 = bf16[1,1,32,2048]{3,0,2,1:T(2,128)(2,1)S(1)} collective-permute-done((bf16[1,1,32,2048]{3,0,2,1:T(2,128)(2,1)S(1)}, bf16[1,1,32,2048]{3,0,2,1:T(2,128)(2,1)S(1)}, u32[]{:S(2)}, u32[]{:S(2)}) %collective-permute-start.4) | collective-permute-done | bytes 131104 | tf_op jit(solution)/shard_map/ppermute | solution.py:18
  100.5 6.0 %collective-permute-done.6 = bf16[1,1,32,2048]{3,0,2,1:T(2,128)(2,1)S(1)} collective-permute-done((bf16[1,1,32,2048]{3,0,2,1:T(2,128)(2,1)S(1)}, bf16[1,1,32,2048]{3,0,2,1:T(2,128)(2,1)S(1)}, u32[]{:S(2)}, u32[]{:S(2)}) %collective-permute-start.6) | collective-permute-done | bytes 131104 | tf_op jit(solution)/shard_map/ppermute | solution.py:18
  106.6 1.0 copy-done.6
  (46 shorter events, 5.4 us)
Async XLA Ops:
  7.2 42.1 %copy-start = (f32[1,32,2048]{2,1,0:T(8,128)S(1)}, f32[1,32,2048]{2,1,0:T(8,128)}, u32[]{:S(2)}) copy-start(f32[1,32,2048]{2,1,0:T(8,128)} %param.8) | copy-start | bytes 786436
  7.2 2.9 %copy-start.7 = (s32[1,32]{1,0:T(1,128)S(1)}, s32[1,32]{1,0:T(1,128)}, u32[]{:S(2)}) copy-start(s32[1,32]{1,0:T(1,128)} %param.7) | copy-start | bytes 388
  7.2 3.0 %copy-start.1 = (f32[1,32]{1,0:T(1,128)S(1)}, f32[1,32]{1,0:T(1,128)}, u32[]{:S(2)}) copy-start(f32[1,32]{1,0:T(1,128)} %param.12) | copy-start | bytes 388
  7.2 63.2 %reduce-scatter.2.cloned.1.call-start = ((), (), s32[]{:S(2)}) async-start(), calls=%async_computation.6 | async-start | bytes 2359296 | tf_op jit(solution)/shard_map/reduce_scatter | solution.py:62
  10.1 8.8 %copy-start.3 = (bf16[1,32,2048]{2,1,0:T(8,128)(2,1)S(1)}, bf16[1,32,2048]{2,1,0:T(8,128)(2,1)}, u32[]{:S(2)}) copy-start(bf16[1,32,2048]{2,1,0:T(8,128)(2,1)} %param.11) | copy-start | bytes 393220
  10.1 9.5 %copy-start.2 = (f32[1,32]{1,0:T(1,128)S(1)}, f32[1,32]{1,0:T(1,128)}, u32[]{:S(2)}) copy-start(f32[1,32]{1,0:T(1,128)} %param.10) | copy-start | bytes 388
  10.1 28.2 %copy-start.4 = (bf16[1,32,2048]{2,1,0:T(8,128)(2,1)S(1)}, bf16[1,32,2048]{2,1,0:T(8,128)(2,1)}, u32[]{:S(2)}) copy-start(bf16[1,32,2048]{2,1,0:T(8,128)(2,1)} %param.9) | copy-start | bytes 393220
  11.6 14.5 %all-to-all-start.4 = ((f32[32,1,1]{2,1,0:T(1,128)}), f32[32,1,1]{2,1,0:T(1,128)S(1)}, u32[]{:S(2)}, u32[]{:S(2)}) async-start(f32[32,1,1]{2,1,0:T(1,128)} %copy.55), calls=%async_computation.5 | async-start | bytes 32768 | tf_op jit(solution)/shard_map/all_to_all | solution.py:55
  26.0 9.7 %all-to-all-start.2 = ((f32[32,1,1]{2,1,0:T(1,128)}), f32[32,1,1]{2,1,0:T(1,128)S(1)}, u32[]{:S(2)}, u32[]{:S(2)}) async-start(f32[32,1,1]{2,1,0:T(1,128)} %copy.52), calls=%async_computation.2 | async-start | bytes 32768 | tf_op jit(solution)/shard_map/all_to_all | solution.py:51
  35.7 11.0 %all-to-all-start.3 = ((bf16[32,2,1024]{2,1,0:T(2,128)(2,1)}), bf16[32,2,1024]{2,1,0:T(2,128)(2,1)S(1)}, u32[]{:S(2)}, u32[]{:S(2)}) async-start(bf16[32,2,1024]{2,1,0:T(2,128)(2,1)} %reshape.649), calls=%async_computation.4 | async-start | bytes 262144 | tf_op jit(solution)/shard_map/all_to_all | solution.py:52
  46.7 11.0 %all-to-all-start.1 = ((bf16[32,2,1024]{2,1,0:T(2,128)(2,1)}), bf16[32,2,1024]{2,1,0:T(2,128)(2,1)S(1)}, u32[]{:S(2)}, u32[]{:S(2)}) async-start(bf16[32,2,1024]{2,1,0:T(2,128)(2,1)} %reshape.647), calls=%async_computation.1 | async-start | bytes 262144 | tf_op jit(solution)/shard_map/all_to_all | solution.py:48
  57.6 12.8 %all-to-all-start = ((f32[32,1,2048]{2,1,0:T(1,128)}), f32[32,1,2048]{2,1,0:T(1,128)S(1)}, u32[]{:S(2)}, u32[]{:S(2)}) async-start(f32[32,1,2048]{2,1,0:T(1,128)} %copy.49), calls=%async_computation | async-start | bytes 524288 | tf_op jit(solution)/shard_map/all_to_all | solution.py:47
  70.4 7.3 %copy-start.5 = (f32[1,1,1,32,2048]{4,3,1,0,2:T(8,128)S(1)}, f32[1,1,1,32,2048]{4,3,1,0,2:T(8,128)}, u32[]{:S(2)}) copy-start(f32[1,1,1,32,2048]{4,3,1,0,2:T(8,128)} %reduce-scatter.2.cloned.1.call-done) | copy-start | bytes 786436
  73.2 9.2 %collective-permute-start = (bf16[1,1,32,2048]{3,0,2,1:T(2,128)(2,1)S(1)}, bf16[1,1,32,2048]{3,0,2,1:T(2,128)(2,1)S(1)}, u32[]{:S(2)}, u32[]{:S(2)}) collective-permute-start(bf16[1,1,32,2048]{3,0,2,1:T(2,128)(2,1)S(1)} %fusion.24), channel_id=1, source_target_pairs={{0,4},{4,8},{8,12},{12,16},{16,20},{20,24},{24,28},{28,0},{1,5},{5... | collective-permute-start | bytes 393224 | tf_op jit(solution)/shard_map/ppermute | solution.py:18
  73.6 8.8 %collective-permute-start.1 = (bf16[1,1,32,2048]{3,0,2,1:T(2,128)(2,1)S(1)}, bf16[1,1,32,2048]{3,0,2,1:T(2,128)(2,1)S(1)}, u32[]{:S(2)}, u32[]{:S(2)}) collective-permute-start(bf16[1,1,32,2048]{3,0,2,1:T(2,128)(2,1)S(1)} %fusion.24), channel_id=1, source_target_pairs={{0,28},{4,0},{8,4},{12,8},{16,12},{20,16},{24,20},{28,24},{1,29},{... | collective-permute-start | bytes 393224 | tf_op jit(solution)/shard_map/ppermute | solution.py:23
  82.4 9.0 %collective-permute-start.2 = (bf16[1,1,32,2048]{3,0,2,1:T(2,128)(2,1)S(1)}, bf16[1,1,32,2048]{3,0,2,1:T(2,128)(2,1)S(1)}, u32[]{:S(2)}, u32[]{:S(2)}) collective-permute-start(bf16[1,1,32,2048]{3,0,2,1:T(2,128)(2,1)S(1)} %collective-permute-done), channel_id=1, source_target_pairs={{0,4},{4,8},{8,12},{12,16},{16,20},{20,24},{24,28},{28,0},{1,5},{5... | collective-permute-start | bytes 393224 | tf_op jit(solution)/shard_map/ppermute | solution.py:18
  82.5 9.0 %collective-permute-start.3 = (bf16[1,1,32,2048]{3,0,2,1:T(2,128)(2,1)S(1)}, bf16[1,1,32,2048]{3,0,2,1:T(2,128)(2,1)S(1)}, u32[]{:S(2)}, u32[]{:S(2)}) collective-permute-start(bf16[1,1,32,2048]{3,0,2,1:T(2,128)(2,1)S(1)} %collective-permute-done.1), channel_id=1, source_target_pairs={{0,28},{4,0},{8,4},{12,8},{16,12},{20,16},{24,20},{28,24},{1,29},{... | collective-permute-start | bytes 393224 | tf_op jit(solution)/shard_map/ppermute | solution.py:23
  91.4 8.4 %collective-permute-start.4 = (bf16[1,1,32,2048]{3,0,2,1:T(2,128)(2,1)S(1)}, bf16[1,1,32,2048]{3,0,2,1:T(2,128)(2,1)S(1)}, u32[]{:S(2)}, u32[]{:S(2)}) collective-permute-start(bf16[1,1,32,2048]{3,0,2,1:T(2,128)(2,1)S(1)} %collective-permute-done.2), channel_id=1, source_target_pairs={{0,4},{4,8},{8,12},{12,16},{16,20},{20,24},{24,28},{28,0},{1,5},{5... | collective-permute-start | bytes 393224 | tf_op jit(solution)/shard_map/ppermute | solution.py:18
  91.4 9.0 %collective-permute-start.5 = (bf16[1,1,32,2048]{3,0,2,1:T(2,128)(2,1)S(1)}, bf16[1,1,32,2048]{3,0,2,1:T(2,128)(2,1)S(1)}, u32[]{:S(2)}, u32[]{:S(2)}) collective-permute-start(bf16[1,1,32,2048]{3,0,2,1:T(2,128)(2,1)S(1)} %collective-permute-done.3), channel_id=1, source_target_pairs={{0,28},{4,0},{8,4},{12,8},{16,12},{20,16},{24,20},{28,24},{1,29},{... | collective-permute-start | bytes 393224 | tf_op jit(solution)/shard_map/ppermute | solution.py:23
  99.8 6.7 %collective-permute-start.6 = (bf16[1,1,32,2048]{3,0,2,1:T(2,128)(2,1)S(1)}, bf16[1,1,32,2048]{3,0,2,1:T(2,128)(2,1)S(1)}, u32[]{:S(2)}, u32[]{:S(2)}) collective-permute-start(bf16[1,1,32,2048]{3,0,2,1:T(2,128)(2,1)S(1)} %collective-permute-done.4), channel_id=1, source_target_pairs={{0,4},{4,8},{8,12},{12,16},{16,20},{20,24},{24,28},{28,0},{1,5},{5... | collective-permute-start | bytes 393224 | tf_op jit(solution)/shard_map/ppermute | solution.py:18
  106.5 1.0 copy-start.6
Sparse Core Ops, SparseCore 0:
  11.3 46.3 reduce-scatter.1
